TPU v7x, 512 devices: a whole 4x4x16 slice. The times are simulated.
512 devices in a mesh: trainer: 32 (over z_hi, x, y), depth: 16 (over z_lo, core).
Axes of the slice: x: 4, y: 4, z: 16 (z_hi: 2, z_lo: 8; z = z_hi * 8 + z_lo), core: 2. Of those that a mesh axis runs over, the one named last changes fastest.
Arguments:
- noise: bfloat16 [32, 64, 64, 256], P('trainer', 'depth'), may hold values from -6 to 6
- gen_weight: float32 [32, 331776], P('trainer', 'depth'), may hold values from -0.15625 to 0.15625
- gen_momentum: float32 [32, 331776], P('trainer', 'depth'), may hold values from -6 to 6
- disc_weight: bfloat16 [32, 8, 128, 64], P('trainer'), may hold values from -0.25 to 0.25
- score_weight: float32 [32, 128], P('trainer'), may hold values from -0.5 to 0.5
- pairing: int32 [32], replicated, may hold values from 0 to 31, as said below
- flags: int32 [32], replicated, may hold values from 0 to 1, as said below
Outputs:
- generated: bfloat16 [32, 64, 64, 256], P('trainer', 'depth')
- new_weight: float32 [32, 331776], P('trainer', 'depth')
- new_momentum: float32 [32, 331776], P('trainer', 'depth')
Inputs may be any that keep to these rules, and one draw needn't show every extreme that they name: pairing is a perfect matching: pairing[pairing[i]] == i and pairing[i] != i for every trainer. `flags`: in every matched pair exactly one trainer has flag 1.
All inputs are finite; a program needn't handle non-finite values.
Results may differ from a plain program's by a relative error of at most 0.013.
Values may be sent and summed in bfloat16 or wider, within the bound.
No kernel may reach another device: no remote copies, remote signals or barrier semaphores. Data moves between devices by JAX's collectives and lax.ppermute only.
A program may use at most 64 MiB of HBM per device.

v0:
```python
import jax
import jax.numpy as jnp
from jax import lax
from jax.sharding import PartitionSpec as P

Y = 2
X = 128
momentum_decay = 0.9
step_length = 0.01


def extended(block, sides, width):
    for axis, dim in sides:
        count = lax.axis_size(axis)
        forward = [(i, i + 1) for i in range(count - 1)]
        backward = [(target, source) for source, target in forward]
        low = lax.ppermute(
            lax.slice_in_dim(block, block.shape[dim] - width, None, axis=dim), axis, forward
        )
        high = lax.ppermute(lax.slice_in_dim(block, 0, width, axis=dim), axis, backward)
        block = jnp.concatenate([low, block, high], axis=dim)
    return block


def framed_copies(padded):
    breadth = X
    cells = padded.shape[2]
    framed = jnp.pad(padded, ((0, 0), (0, 0), (breadth + 1, breadth + 1)))
    column = (jnp.arange(cells + 2 * breadth + 2, dtype=jnp.int32) - breadth - 1) % breadth
    left_copy = jnp.where(
        (column == breadth - 1)[None, None, :], jnp.zeros((), framed.dtype), framed
    )
    right_copy = jnp.where((column == 0)[None, None, :], jnp.zeros((), framed.dtype), framed)
    return (left_copy, framed, right_copy)


def stacked_window(copies, read_y, cells):
    breadth = X
    parts_list = []
    for read_x in range(3):
        begin = read_y * breadth + read_x
        parts_list.append(copies[read_x][:, :, begin : begin + cells])
    return jnp.concatenate(parts_list, axis=1)


def group_kernel(layer):
    channels = layer.shape[-1]
    cube = layer.reshape(3, 3, 3, channels, channels)
    return cube.transpose(0, 1, 3, 2, 4).reshape(3, 3, channels, 3 * channels)


def flip_kernel(layer):
    channels = layer.shape[-1]
    cube = layer.reshape(3, 3, 3, channels, channels)[::-1, ::-1, ::-1].swapaxes(3, 4)
    return cube.transpose(0, 1, 3, 2, 4).reshape(3, 3, channels, 3 * channels)


def convolve_grouped(padded, grouped):
    planes, cells = (padded.shape[0] - 2, padded.shape[2])
    copies = framed_copies(padded)
    summed = jnp.zeros((planes, grouped.shape[2], cells), jnp.float32)
    for read_y in range(3):
        window = stacked_window(copies, read_y, cells)
        for read_z in range(3):
            summed = summed + jnp.einsum(
                "oj,zjs->zos",
                grouped[read_z, read_y],
                window[read_z : read_z + planes],
                preferred_element_type=jnp.float32,
            )
    return summed


def convolve(padded, layer):
    return convolve_grouped(padded, group_kernel(layer))


def convolve_back(padded, layer):
    return convolve_grouped(padded, flip_kernel(layer))


def kernel_grad(gradient, padded):
    planes, channels_out, cells = gradient.shape
    channels_in = padded.shape[1]
    copies = framed_copies(padded)
    rows_list = []
    for read_z in range(3):
        row_list = []
        for read_y in range(3):
            window = stacked_window(copies, read_y, cells)
            row_list.append(
                jnp.einsum(
                    "zos,zjs->oj",
                    gradient,
                    window[read_z : read_z + planes],
                    preferred_element_type=jnp.float32,
                )
            )
        rows_list.append(jnp.stack(row_list))
    grouped = jnp.stack(rows_list)
    return (
        grouped.reshape(3, 3, channels_out, 3, channels_in)
        .transpose(0, 1, 3, 2, 4)
        .reshape(27, channels_out, channels_in)
    )


def gelu_back(inputs, upstream):
    return jax.vjp(jax.nn.gelu, inputs)[1](upstream)[0]


def widen_back(gradient):
    return extended(gradient, (("depth", 0),), 1)


def widen_forward(volume):
    return extended(volume, (("depth", 0),), 1)


def critic_grad(generated, disc_kernel, score_vector):
    planes, channels, cells = generated.shape
    blocks = generated.reshape(planes // 2, 2, channels, Y // 2, 2, X // 2, 2)
    kernel_cube = disc_kernel.reshape(2, 2, 2, disc_kernel.shape[1], channels)
    response = jnp.einsum(
        "abdoc,zacybxd->zoyx", kernel_cube, blocks, preferred_element_type=jnp.float32
    )
    features = jax.nn.gelu(response)
    scores = jnp.sum(score_vector[None, :, None, None] * features, axis=1)
    slope = -jax.nn.sigmoid(-scores)
    upstream = gelu_back(response, slope[:, None] * score_vector[None, :, None, None]).astype(
        jnp.bfloat16
    )
    spread = jnp.einsum(
        "abdoc,zoyx->zacybxd", kernel_cube, upstream, preferred_element_type=jnp.float32
    )
    return spread.reshape(planes, channels, cells)


def on_device(noise, gen_weight, gen_momentum, disc_weight, score_weight, pairing, flags):
    trainer_rank = lax.axis_index("trainer")
    partner = pairing[trainer_rank]
    keeper = flags[trainer_rank] == 1
    pieces_in = (
        lax.all_gather(gen_weight.astype(jnp.bfloat16), "trainer", axis=0, tiled=True).astype(
            jnp.float32
        ),
        lax.all_gather(gen_momentum.astype(jnp.bfloat16), "trainer", axis=0, tiled=True).astype(
            jnp.float32
        ),
    )
    row_ids = jnp.arange(pieces_in[0].shape[0], dtype=jnp.int32)
    matched = (row_ids == partner)[:, None]
    weight_part = jnp.sum(jnp.where(matched, pieces_in[0], 0.0), axis=0, keepdims=True)
    moment_part = jnp.sum(jnp.where(matched, pieces_in[1], 0.0), axis=0, keepdims=True)
    other_weight = jnp.zeros_like(gen_weight) + weight_part
    other_moment = jnp.zeros_like(gen_momentum) + moment_part
    chosen_weight = jnp.where(keeper, gen_weight, other_weight)
    chosen_momentum = jnp.where(keeper, gen_momentum, other_moment)
    channels = noise.shape[2]
    all_kernels = lax.all_gather(chosen_weight.astype(jnp.bfloat16), "depth", axis=1, tiled=True)
    layers = all_kernels.reshape(3, 27, channels, channels)
    latent = noise[0]
    latent_pad = widen_forward(latent)
    first_pre = convolve(latent_pad, layers[0])
    first_act_pad = widen_forward(jax.nn.gelu(first_pre).astype(jnp.bfloat16))
    second_pre = convolve(first_act_pad, layers[1])
    second_act_pad = widen_forward(jax.nn.gelu(second_pre).astype(jnp.bfloat16))
    third_pre = convolve(second_act_pad, layers[2])
    output_f = jnp.tanh(third_pre)
    generated = output_f.astype(jnp.bfloat16)
    gen_grad = critic_grad(generated, disc_weight[0], score_weight[0])
    third_grad = (gen_grad * (1.0 - output_f * output_f)).astype(jnp.bfloat16)
    grad_three = kernel_grad(third_grad, second_act_pad)
    second_back = convolve_back(widen_back(third_grad), layers[2])
    second_grad = gelu_back(second_pre, second_back).astype(jnp.bfloat16)
    grad_two = kernel_grad(second_grad, first_act_pad)
    first_back = convolve_back(widen_back(second_grad), layers[1])
    first_grad = gelu_back(first_pre, first_back).astype(jnp.bfloat16)
    grad_one = kernel_grad(first_grad, latent_pad)
    local_grad = jnp.concatenate(
        [grad_one.reshape(-1), grad_two.reshape(-1), grad_three.reshape(-1)]
    )
    share_len = gen_weight.shape[1]
    grad_whole = lax.psum(local_grad.astype(jnp.bfloat16), "depth").astype(jnp.float32)
    grad_share = lax.dynamic_slice_in_dim(
        grad_whole, lax.axis_index("depth") * share_len, share_len, 0
    )
    new_momentum = momentum_decay * chosen_momentum + grad_share[None, :]
    new_weight = chosen_weight - step_length * new_momentum
    return (generated[None], new_weight, new_momentum)


def solution(mesh):
    placed = (
        P("trainer", "depth", None, None),
        P("trainer", "depth"),
        P("trainer", "depth"),
        P("trainer", None, None, None),
        P("trainer", None),
        P(),
        P(),
    )
    return jax.shard_map(
        on_device,
        mesh=mesh,
        in_specs=placed,
        out_specs=(P("trainer", "depth", None, None), P("trainer", "depth"), P("trainer", "depth")),
        check_vma=False,
    )
```

profile of v0, /device:TPU:1, one launch (start us, length us, event | category | flops | bytes accessed | tf_op | source)
XLA Modules:
  0.0 621.0 jit_solution(14482769151043284614)
XLA Ops:
  11.4 4.9 collective-permute-start
  16.3 5.1 collective-permute-start.1
  28.7 124.7 %all-gather.5.cloned.1.call-done = bf16[32,1,20736]{2,1,0:T(2,128)(2,1)} async-done(((bf16[1,1,20736]{2,1,0:T(2,128)(2,1)}), bf16[32,1,20736]{2,1,0:T(2,128)(2,1)}) %all-gather.5.cloned.1.call-update) | async-done | bytes 1327120 | tf_op jit(solution)/shard_map/all_gather | solution.py:144
  153.4 4.5 convert_element_type.63
  157.9 131.5 %all-gather.7.cloned.1.call-done = bf16[32,1,20736]{2,1,0:T(2,128)(2,1)} async-done(((bf16[1,1,20736]{2,1,0:T(2,128)(2,1)}), bf16[32,1,20736]{2,1,0:T(2,128)(2,1)}) %all-gather.7.cloned.1.call-update) | async-done | bytes 1327120 | tf_op jit(solution)/shard_map/all_gather | solution.py:147
  289.4 3.2 fusion.1
  293.2 39.0 %all_gather.10 = bf16[1,331776]{1,0:T(2,128)(2,1)S(1)} all-gather(bf16[1,20736]{1,0:T(2,128)(2,1)S(1)} %fusion.167), channel_id=1, replica_groups=mesh['trainer'=32,'depth'=16] {'depth'}, dimensions={1}, use_global_device_ids=true | all-gather | bytes 705024 | tf_op jit(solution)/shard_map/all_gather | solution.py:160
  332.2 4.4 slice_reduce_fusion.2
  340.9 1.9 collective-permute-start.2
  342.8 2.6 collective-permute-start.3
  352.5 1.9 collective-permute-start.4
  354.4 2.4 collective-permute-start.5
  358.6 1.9 reshape_squeeze.16
  360.5 1.8 rev.6
  362.4 2.0 copy.119
  373.0 1.9 copy.133
  386.3 3.1 collective-permute-start.6
  389.5 1.9 collective-permute-start.7
  393.2 2.0 copy.181
  395.1 2.0 reshape_reshape.14
  406.4 3.6 collective-permute-start.8
  410.0 2.1 collective-permute-start.9
  413.5 1.9 collective-permute-done.9
  426.5 186.2 %all-reduce.7.cloned.1.call-done = bf16[331776]{0:T(1024)(128)(2,1)} async-done(((bf16[331776]{0:T(1024)(128)(2,1)}), bf16[331776]{0:T(1024)(128)(2,1)}) %all-reduce.7.cloned.1.call-update) | async-done | bytes 663568 | tf_op jit(solution)/shard_map/psum | solution.py:184
  (249 shorter events, 68.9 us)
Async XLA Ops:
  7.2 363.0 %copy-start = (bf16[1,8,128,64]{2,3,1,0:T(8,128)(2,1)S(1)}, bf16[1,8,128,64]{2,3,1,0:T(8,128)(2,1)}, u32[]{:S(2)}) copy-start(bf16[1,8,128,64]{2,3,1,0:T(8,128)(2,1)} %param.10) | copy-start | bytes 393220
  7.2 146.2 %all-gather.5.cloned.1.call-start = ((), (), s32[]{:S(2)}) async-start(), calls=%async_computation.1 | async-start | bytes 2737152 | tf_op jit(solution)/shard_map/all_gather | solution.py:144
  8.9 280.5 %all-gather.7.cloned.1.call-start = ((), (), s32[]{:S(2)}) async-start(), calls=%async_computation.2 | async-start | bytes 2737152 | tf_op jit(solution)/shard_map/all_gather | solution.py:147
  10.5 602.1 %all-reduce.7.cloned.1.call-start = ((), (), s32[]{:S(2)}) async-start(), calls=%async_computation | async-start | bytes 1327104 | tf_op jit(solution)/shard_map/psum | solution.py:184
  11.4 13.9 %collective-permute-start = (bf16[1,64,256]{2,1,0:T(8,128)(2,1)S(1)}, bf16[1,64,256]{2,1,0:T(8,128)(2,1)S(1)}, u32[]{:S(2)}, u32[]{:S(2)}) collective-permute-start(bf16[1,64,256]{2,1,0:T(8,128)(2,1)S(1)} %get-tuple-element.73), channel_id=1, source_target_pairs={{0,1},{1,2},{2,3},{3,4},{4,5},{5,6},{6,7},{7,8},{8,9},{9,10},{10,1... | collective-permute-start | bytes 98312 | tf_op jit(solution)/shard_map/ppermute | solution.py:17
  16.3 9.0 %collective-permute-start.1 = (bf16[1,64,256]{2,1,0:T(8,128)(2,1)S(1)}, bf16[1,64,256]{2,1,0:T(8,128)(2,1)S(1)}, u32[]{:S(2)}, u32[]{:S(2)}) collective-permute-start(bf16[1,64,256]{2,1,0:T(8,128)(2,1)S(1)} %get-tuple-element.74), channel_id=1, source_target_pairs={{1,0},{2,1},{3,2},{4,3},{5,4},{6,5},{7,6},{8,7},{9,8},{10,9},{11,1... | collective-permute-start | bytes 98312 | tf_op jit(solution)/shard_map/ppermute | solution.py:20
  22.7 341.7 %copy-start.27 = (pred[514]{0:T(1024)(128)(4,1)}, pred[514]{0:T(1024)(128)(4,1)S(1)}, u32[]{:S(2)}) copy-start(pred[514]{0:T(1024)(128)(4,1)S(1)} %broadcast_compare_fusion.1) | copy-start | bytes 1546
  22.7 341.7 %copy-start.29 = (pred[514]{0:T(1024)(128)(4,1)}, pred[514]{0:T(1024)(128)(4,1)S(1)}, u32[]{:S(2)}) copy-start(pred[514]{0:T(1024)(128)(4,1)S(1)} %broadcast_compare_fusion) | copy-start | bytes 1546
  157.9 134.7 %copy-start.21 = (f32[1,20736]{1,0:T(1,128)S(1)}, f32[1,20736]{1,0:T(1,128)}, u32[]{:S(2)}) copy-start(f32[1,20736]{1,0:T(1,128)} %param.8) | copy-start | bytes 248836
  340.9 5.7 collective-permute-start.2
  342.8 5.2 collective-permute-start.3
  345.6 3.3 copy-start.11
  352.5 11.8 %collective-permute-start.4 = (bf16[1,64,256]{2,1,0:T(8,128)(2,1)S(1)}, bf16[1,64,256]{2,1,0:T(8,128)(2,1)S(1)}, u32[]{:S(2)}, u32[]{:S(2)}) collective-permute-start(bf16[1,64,256]{2,1,0:T(8,128)(2,1)S(1)} %get-tuple-element.69), channel_id=1, source_target_pairs={{0,1},{1,2},{2,3},{3,4},{4,5},{5,6},{6,7},{7,8},{8,9},{9,10},{10,1... | collective-permute-start | bytes 98312 | tf_op jit(solution)/shard_map/ppermute | solution.py:17
  354.4 9.9 %collective-permute-start.5 = (bf16[1,64,256]{2,1,0:T(8,128)(2,1)S(1)}, bf16[1,64,256]{2,1,0:T(8,128)(2,1)S(1)}, u32[]{:S(2)}, u32[]{:S(2)}) collective-permute-start(bf16[1,64,256]{2,1,0:T(8,128)(2,1)S(1)} %get-tuple-element.70), channel_id=1, source_target_pairs={{1,0},{2,1},{3,2},{4,3},{5,4},{6,5},{7,6},{8,7},{9,8},{10,9},{11,1... | collective-permute-start | bytes 98312 | tf_op jit(solution)/shard_map/ppermute | solution.py:20
  386.3 10.8 %collective-permute-start.6 = (bf16[1,64,256]{2,1,0:T(8,128)(2,1)}, bf16[1,64,256]{2,1,0:T(8,128)(2,1)}, u32[]{:S(2)}, u32[]{:S(2)}) collective-permute-start(bf16[1,64,256]{2,1,0:T(8,128)(2,1)} %get-tuple-element.67), channel_id=1, source_target_pairs={{0,1},{1,2},{2,3},{3,4},{4,5},{5,6},{6,7},{7,8},{8,9},{9,10},{10,1... | collective-permute-start | bytes 98312 | tf_op jit(solution)/shard_map/ppermute | solution.py:17
  389.5 7.6 %collective-permute-start.7 = (bf16[1,64,256]{2,1,0:T(8,128)(2,1)}, bf16[1,64,256]{2,1,0:T(8,128)(2,1)}, u32[]{:S(2)}, u32[]{:S(2)}) collective-permute-start(bf16[1,64,256]{2,1,0:T(8,128)(2,1)} %get-tuple-element.68), channel_id=1, source_target_pairs={{1,0},{2,1},{3,2},{4,3},{5,4},{6,5},{7,6},{8,7},{9,8},{10,9},{11,1... | collective-permute-start | bytes 98312 | tf_op jit(solution)/shard_map/ppermute | solution.py:20
  393.2 4.0 copy-start.28
  393.2 4.0 copy-start.30
  406.4 7.1 %collective-permute-start.8 = (bf16[1,64,256]{2,1,0:T(8,128)(2,1)S(1)}, bf16[1,64,256]{2,1,0:T(8,128)(2,1)S(1)}, u32[]{:S(2)}, u32[]{:S(2)}) collective-permute-start(bf16[1,64,256]{2,1,0:T(8,128)(2,1)S(1)} %get-tuple-element.65), channel_id=1, source_target_pairs={{0,1},{1,2},{2,3},{3,4},{4,5},{5,6},{6,7},{7,8},{8,9},{9,10},{10,1... | collective-permute-start | bytes 98312 | tf_op jit(solution)/shard_map/ppermute | solution.py:17
  410.0 5.3 collective-permute-start.9
  425.5 188.0 %copy-start.20 = (f32[20736]{0:T(1024)S(1)}, f32[20736]{0:T(1024)}, u32[]{:S(2)}) copy-start(f32[20736]{0:T(1024)} %copy-done.19) | copy-start | bytes 248836
  425.5 188.0 %copy-start.22 = (f32[1,20736]{1,0:T(1,128)S(1)}, f32[1,20736]{1,0:T(1,128)}, u32[]{:S(2)}) copy-start(f32[1,20736]{1,0:T(1,128)} %param.8) | copy-start | bytes 248836
  425.6 188.0 %copy-start.23 = (f32[20736]{0:T(1024)S(1)}, f32[20736]{0:T(1024)}, u32[]{:S(2)}) copy-start(f32[20736]{0:T(1024)} %get-tuple-element.6) | copy-start | bytes 248836
  425.6 188.0 %copy-start.24 = (f32[1,20736]{1,0:T(1,128)S(1)}, f32[1,20736]{1,0:T(1,128)}, u32[]{:S(2)}) copy-start(f32[1,20736]{1,0:T(1,128)} %param.9) | copy-start | bytes 248836
  (21 other events, 26.8 us)
Sparse Core Ops, SparseCore 0:
  12.8 140.5 all-gather.4
  158.2 131.0 all-gather.6
  426.6 186.0 all-reduce.6
where the time goes:
time: 623 us; the launch traced here: 621 us
  waiting for transfers between devices  446 us (72%)
  local copies, waits for them, and re-layouts  42.4 us (7%)
  blocking collectives  39 us (6%)
  starting transfers between devices  29.8 us (5%)
  other arithmetic  25.9 us (4%)
  matrix products  22.7 us (4%)
  between operations  15.6 us (3%)
    psum x1, waiting for transfers between devices, on_device(): lax.psum(local_grad.astype(jnp.bfloat16), 'depth').astype(jnp.float32)  186 us
    all_gather x1, waiting for transfers between devices, on_device(): lax.all_gather(gen_momentum.astype(jnp.bfloat16), 'trainer', axis=0, tile...  131 us
    all_gather x1, waiting for transfers between devices, on_device(): lax.all_gather(gen_weight.astype(jnp.bfloat16), 'trainer', axis=0, tiled=...  125 us
    all_gather x1, blocking collectives, on_device(): lax.all_gather(chosen_weight.astype(jnp.bfloat16), 'depth', axis=1, tiled...  39 us
    ppermute x5, starting transfers between devices, extended(): lax.ppermute(lax.slice_in_dim(block, block.shape[dim] - width, None, axis...  15.5 us
    ppermute x5, starting transfers between devices, extended(): lax.ppermute(lax.slice_in_dim(block, 0, width, axis=dim), axis, backward)  14.2 us
  transfers between devices with their start and end apart: 13, of which 5 were waited for; matrix products, arithmetic and copies ran while one was open for 5% of the time, Pallas kernels for 0%

commit v1 on v0

--- a/solution.py
+++ b/solution.py
@@ -181,7 +181,9 @@
         [grad_one.reshape(-1), grad_two.reshape(-1), grad_three.reshape(-1)]
     )
     share_len = gen_weight.shape[1]
-    grad_whole = lax.psum(local_grad.astype(jnp.bfloat16), "depth").astype(jnp.float32)
+    grad_whole = jnp.sum(lax.all_gather(local_grad.astype(jnp.bfloat16), "depth"), axis=0).astype(
+        jnp.float32
+    )
     grad_share = lax.dynamic_slice_in_dim(
         grad_whole, lax.axis_index("depth") * share_len, share_len, 0
     )

time: 623 us -> 782 us (1.26); the launches traced: 621 us -> 770 us
  other arithmetic: 25.9 us -> 146 us
  waiting for transfers between devices: 446 us -> 480 us
    all_gather x0 -> x1, waiting for transfers between devices: none -> 220 us  [on_device(): lax.all_gather(local_grad.astype(jnp.bfloat16), 'depth')]
    psum x1 -> x0, waiting for transfers between devices: 186 us -> none  [on_device(): lax.psum(local_grad.astype(jnp.bfloat16), 'depth').astype(jnp.float32)]
    reduce_sum x0 -> x1, other arithmetic: none -> 111 us  [on_device(): jnp.sum(lax.all_gather(local_grad.astype(jnp.bfloat16), 'depth'), axis=0)]
    unnamed x2 -> x3, other arithmetic: 3.19 us -> 16.3 us
  transfers between devices with their start and end apart: 13 -> 13, of which waited for: 5 -> 5; matrix products, arithmetic and copies ran while one was open for 5% -> 4% of each run, Pallas kernels for 0% -> 0%
where the time goes in v1:
time: 782 us; the launch traced here: 770 us
  waiting for transfers between devices  480 us (61%)
  other arithmetic  146 us (19%)
  blocking collectives  39 us (5%)
  local copies, waits for them, and re-layouts  38.2 us (5%)
  starting transfers between devices  29.8 us (4%)
  matrix products  21.9 us (3%)
  between operations  15.6 us (2%)
    all_gather x1, waiting for transfers between devices, on_device(): lax.all_gather(local_grad.astype(jnp.bfloat16), 'depth')  220 us
    all_gather x1, waiting for transfers between devices, on_device(): lax.all_gather(gen_momentum.astype(jnp.bfloat16), 'trainer', axis=0, tile...  131 us
    all_gather x1, waiting for transfers between devices, on_device(): lax.all_gather(gen_weight.astype(jnp.bfloat16), 'trainer', axis=0, tiled=...  125 us
    reduce_sum x1, other arithmetic, on_device(): jnp.sum(lax.all_gather(local_grad.astype(jnp.bfloat16), 'depth'), axis=0)  111 us
    all_gather x1, blocking collectives, on_device(): lax.all_gather(chosen_weight.astype(jnp.bfloat16), 'depth', axis=1, tiled...  39 us
    unnamed x3, other arithmetic  16.3 us
  transfers between devices with their start and end apart: 13, of which 5 were waited for; matrix products, arithmetic and copies ran while one was open for 4% of the time, Pallas kernels for 0%

profile of v1, /device:TPU:1, one launch (start us, length us, event | category | flops | bytes accessed | tf_op | source)
XLA Modules:
  0.0 769.9 jit_solution(1725099222217264566)
XLA Ops:
  11.4 4.9 collective-permute-start
  16.3 5.1 collective-permute-start.1
  28.7 124.7 %all-gather.7.cloned.1.call-done = bf16[32,1,20736]{2,1,0:T(2,128)(2,1)} async-done(((bf16[1,1,20736]{2,1,0:T(2,128)(2,1)}), bf16[32,1,20736]{2,1,0:T(2,128)(2,1)}) %all-gather.7.cloned.1.call-update) | async-done | bytes 1327120 | tf_op jit(solution)/shard_map/all_gather | solution.py:144
  153.4 4.5 convert_element_type.72
  157.9 131.5 %all-gather.9.cloned.1.call-done = bf16[32,1,20736]{2,1,0:T(2,128)(2,1)} async-done(((bf16[1,1,20736]{2,1,0:T(2,128)(2,1)}), bf16[32,1,20736]{2,1,0:T(2,128)(2,1)}) %all-gather.9.cloned.1.call-update) | async-done | bytes 1327120 | tf_op jit(solution)/shard_map/all_gather | solution.py:147
  289.4 3.2 fusion.1
  293.2 39.0 %all_gather.14 = bf16[1,331776]{1,0:T(2,128)(2,1)S(1)} all-gather(bf16[1,20736]{1,0:T(2,128)(2,1)S(1)} %fusion.167), channel_id=1, replica_groups=mesh['trainer'=32,'depth'=16] {'depth'}, dimensions={1}, use_global_device_ids=true | all-gather | bytes 705024 | tf_op jit(solution)/shard_map/all_gather | solution.py:160
  332.2 4.4 slice_reduce_fusion.2
  342.8 2.6 collective-permute-start.3
  352.5 1.9 collective-permute-start.4
  354.4 2.4 collective-permute-start.5
  358.6 1.9 reshape_squeeze.16
  362.4 2.0 copy.119
  372.8 1.9 copy.133
  381.9 3.2 collective-permute-start.6
  385.1 1.9 collective-permute-start.7
  387.9 2.0 copy.181
  389.9 2.0 concatenate.150
  401.2 3.6 collective-permute-start.8
  404.8 2.1 collective-permute-start.9
  407.6 2.4 collective-permute-done.9
  418.7 13.1 %maximum_bitcast_fusion = bf16[1,1,331776]{2,1,0:T(2,128)(2,1)} fusion(bf16[1,110592]{1,0:T(2,128)(2,1)S(1)} %copy-done.13, bf16[1,110592]{1,0:T(2,128)(2,1)S(1)} %concatenate.149, bf16[1,110592]{1,0:T(2,128)(2,1)S(1)} %concatenate.148), kind=kLoop, calls=%fused_computation.6 | loop fusion | flops 1990656 | bytes 1327104
  431.9 219.7 %all-gather.11.cloned.1.call-done = bf16[16,1,331776]{2,1,0:T(2,128)(2,1)} async-done(((bf16[1,1,331776]{2,1,0:T(2,128)(2,1)}), bf16[16,1,331776]{2,1,0:T(2,128)(2,1)}) %all-gather.11.cloned.1.call-update) | async-done | bytes 10616848 | tf_op jit(solution)/shard_map/all_gather | solution.py:184
  651.6 110.7 %reduce_sum.42 = bf16[331776]{0:T(1024)(128)(2,1)S(1)} reduce(bf16[16,1,331776]{2,1,0:T(2,128)(2,1)} %all-gather.11.cloned.1.call-done, bf16[]{:T(256)} %constant.76.clone.1), dimensions={0,1}, to_apply=%region_3.4 | reduce | flops 4976640 | bytes 11280386 | tf_op jit(solution)/shard_map/reduce_sum | solution.py:184
  (250 shorter events, 63.5 us)
Async XLA Ops:
  7.2 362.8 %copy-start = (bf16[1,8,128,64]{2,3,1,0:T(8,128)(2,1)S(1)}, bf16[1,8,128,64]{2,3,1,0:T(8,128)(2,1)}, u32[]{:S(2)}) copy-start(bf16[1,8,128,64]{2,3,1,0:T(8,128)(2,1)} %param.10) | copy-start | bytes 393220
  7.2 146.2 %all-gather.7.cloned.1.call-start = ((), (), s32[]{:S(2)}) async-start(), calls=%async_computation | async-start | bytes 2737152 | tf_op jit(solution)/shard_map/all_gather | solution.py:144
  8.9 280.5 %all-gather.9.cloned.1.call-start = ((), (), s32[]{:S(2)}) async-start(), calls=%async_computation.1 | async-start | bytes 2737152 | tf_op jit(solution)/shard_map/all_gather | solution.py:147
  10.5 641.1 %all-gather.11.cloned.1.call-start = ((), (), s32[]{:S(2)}) async-start(), calls=%async_computation.2 | async-start | bytes 22560768 | tf_op jit(solution)/shard_map/all_gather | solution.py:184
  11.4 13.9 %collective-permute-start = (bf16[1,64,256]{2,1,0:T(8,128)(2,1)S(1)}, bf16[1,64,256]{2,1,0:T(8,128)(2,1)S(1)}, u32[]{:S(2)}, u32[]{:S(2)}) collective-permute-start(bf16[1,64,256]{2,1,0:T(8,128)(2,1)S(1)} %get-tuple-element.73), channel_id=1, source_target_pairs={{0,1},{1,2},{2,3},{3,4},{4,5},{5,6},{6,7},{7,8},{8,9},{9,10},{10,1... | collective-permute-start | bytes 98312 | tf_op jit(solution)/shard_map/ppermute | solution.py:17
  16.3 9.0 %collective-permute-start.1 = (bf16[1,64,256]{2,1,0:T(8,128)(2,1)S(1)}, bf16[1,64,256]{2,1,0:T(8,128)(2,1)S(1)}, u32[]{:S(2)}, u32[]{:S(2)}) collective-permute-start(bf16[1,64,256]{2,1,0:T(8,128)(2,1)S(1)} %get-tuple-element.74), channel_id=1, source_target_pairs={{1,0},{2,1},{3,2},{4,3},{5,4},{6,5},{7,6},{8,7},{9,8},{10,9},{11,1... | collective-permute-start | bytes 98312 | tf_op jit(solution)/shard_map/ppermute | solution.py:20
  22.7 341.7 %copy-start.27 = (pred[514]{0:T(1024)(128)(4,1)}, pred[514]{0:T(1024)(128)(4,1)S(1)}, u32[]{:S(2)}) copy-start(pred[514]{0:T(1024)(128)(4,1)S(1)} %broadcast_compare_fusion.1) | copy-start | bytes 1546
  22.7 341.7 %copy-start.29 = (pred[514]{0:T(1024)(128)(4,1)}, pred[514]{0:T(1024)(128)(4,1)S(1)}, u32[]{:S(2)}) copy-start(pred[514]{0:T(1024)(128)(4,1)S(1)} %broadcast_compare_fusion) | copy-start | bytes 1546
  157.9 134.7 %copy-start.21 = (f32[1,20736]{1,0:T(1,128)S(1)}, f32[1,20736]{1,0:T(1,128)}, u32[]{:S(2)}) copy-start(f32[1,20736]{1,0:T(1,128)} %param.8) | copy-start | bytes 248836
  340.9 5.7 collective-permute-start.2
  342.8 5.2 collective-permute-start.3
  352.5 11.9 %collective-permute-start.4 = (bf16[1,64,256]{2,1,0:T(8,128)(2,1)S(1)}, bf16[1,64,256]{2,1,0:T(8,128)(2,1)S(1)}, u32[]{:S(2)}, u32[]{:S(2)}) collective-permute-start(bf16[1,64,256]{2,1,0:T(8,128)(2,1)S(1)} %get-tuple-element.69), channel_id=1, source_target_pairs={{0,1},{1,2},{2,3},{3,4},{4,5},{5,6},{6,7},{7,8},{8,9},{9,10},{10,1... | collective-permute-start | bytes 98312 | tf_op jit(solution)/shard_map/ppermute | solution.py:17
  354.4 9.9 %collective-permute-start.5 = (bf16[1,64,256]{2,1,0:T(8,128)(2,1)S(1)}, bf16[1,64,256]{2,1,0:T(8,128)(2,1)S(1)}, u32[]{:S(2)}, u32[]{:S(2)}) collective-permute-start(bf16[1,64,256]{2,1,0:T(8,128)(2,1)S(1)} %get-tuple-element.70), channel_id=1, source_target_pairs={{1,0},{2,1},{3,2},{4,3},{5,4},{6,5},{7,6},{8,7},{9,8},{10,9},{11,1... | collective-permute-start | bytes 98312 | tf_op jit(solution)/shard_map/ppermute | solution.py:20
  381.9 10.0 %collective-permute-start.6 = (bf16[1,64,256]{2,1,0:T(8,128)(2,1)}, bf16[1,64,256]{2,1,0:T(8,128)(2,1)S(1)}, u32[]{:S(2)}, u32[]{:S(2)}) collective-permute-start(bf16[1,64,256]{2,1,0:T(8,128)(2,1)} %get-tuple-element.67), channel_id=1, source_target_pairs={{0,1},{1,2},{2,3},{3,4},{4,5},{5,6},{6,7},{7,8},{8,9},{9,10},{10,1... | collective-permute-start | bytes 98312 | tf_op jit(solution)/shard_map/ppermute | solution.py:17
  385.1 6.9 collective-permute-start.7
  387.9 4.0 copy-start.28
  387.9 4.0 copy-start.30
  401.2 6.4 collective-permute-start.8
  404.8 5.2 collective-permute-start.9
  431.9 330.6 %copy-start.20 = (f32[20736]{0:T(1024)S(1)}, f32[20736]{0:T(1024)}, u32[]{:S(2)}) copy-start(f32[20736]{0:T(1024)} %copy-done.19) | copy-start | bytes 248836
  431.9 330.6 %copy-start.22 = (f32[1,20736]{1,0:T(1,128)S(1)}, f32[1,20736]{1,0:T(1,128)}, u32[]{:S(2)}) copy-start(f32[1,20736]{1,0:T(1,128)} %param.8) | copy-start | bytes 248836
  431.9 330.6 %copy-start.23 = (f32[20736]{0:T(1024)S(1)}, f32[20736]{0:T(1024)}, u32[]{:S(2)}) copy-start(f32[20736]{0:T(1024)} %get-tuple-element.6) | copy-start | bytes 248836
  431.9 330.6 %copy-start.24 = (f32[1,20736]{1,0:T(1,128)S(1)}, f32[1,20736]{1,0:T(1,128)}, u32[]{:S(2)}) copy-start(f32[1,20736]{1,0:T(1,128)} %param.9) | copy-start | bytes 248836
  651.6 111.8 %copy-start.1 = (bf16[1,8,128,64]{2,3,1,0:T(8,128)(2,1)S(1)}, bf16[1,8,128,64]{2,3,1,0:T(8,128)(2,1)}, u32[]{:S(2)}) copy-start(bf16[1,8,128,64]{2,3,1,0:T(8,128)(2,1)} %param.10) | copy-start | bytes 393220
  (21 other events, 32.6 us)
Sparse Core Ops, SparseCore 0:
  12.8 140.5 all-gather.6
  158.2 131.0 all-gather.8
  432.0 219.5 all-gather.10
